TPU v7x, 32 devices: a whole 2x2x4 slice. The times are simulated.
32 devices in a mesh: row: 4 (over x, core), col: 8 (over z, y).
Axes of the slice: x: 2, y: 2, z: 4, core: 2. Of those that a mesh axis runs over, the one named last changes fastest.
Arguments:
- centres: float32 [65536, 64], P(('row', 'col')), may hold values from -6 to 6
- weights: float32 [65536, 64], P(('row', 'col')), may hold values from -0.25 to 0.25
- targets: float32 [512, 64], replicated, may hold values from -6 to 6
- batch_index: int32 [512], replicated, may hold values from 0 to 65535
- nystrom_index: int32 [4096], replicated, may hold values from 0 to 65535
- eigvecs: float32 [4096, 1024], P('row', 'col'), may hold values from -0.09375 to 0.09375
- mode_scale: float32 [1024], P('col'), may hold values from 0.02 to 0.2
Outputs:
- residual: float32 [512, 64], replicated
- step: float32 [65536, 64], P(('row', 'col'))
All inputs are finite; a program needn't handle non-finite values.
Results may differ from a plain program's by a relative error of at most 0.0001.
Values sent between devices are 32-bit elements; how exact they have to be, the bound alone decides.
A program may use at most 128 MiB of HBM per device.

v0:
```python
import jax
import jax.numpy as jnp
from jax import lax
from jax.sharding import PartitionSpec as P

learning_rate = 0.25


def kernel(left, right):
    left_sq = jnp.sum(left * left, axis=1)
    right_sq = jnp.sum(right * right, axis=1)
    inner_prod = jnp.dot(
        left, right.T, precision=lax.Precision.HIGHEST, preferred_element_type=jnp.float32
    )
    return jnp.exp(
        -(left_sq[:, None] + right_sq[None, :] - 2.0 * inner_prod) / float(left.shape[1])
    )


def product(left, right):
    return jnp.dot(left, right, precision=lax.Precision.HIGHEST, preferred_element_type=jnp.float32)


def local(centres, weights, targets, batch_index, nystrom_index, eigvecs, mode_scale):
    rows_dev = centres.shape[0]
    block_rows = eigvecs.shape[0]
    offset = lax.axis_index(("row", "col")) * rows_dev

    def select_rows(index):
        local_rows = index - offset
        inside = (local_rows >= 0) & (local_rows < rows_dev)
        fetched = jnp.take(centres, jnp.clip(local_rows, 0, rows_dev - 1), axis=0)
        return jnp.where(inside[:, None], fetched, 0.0)

    batch_feats, nystrom = lax.psum(
        (select_rows(batch_index), select_rows(nystrom_index)), ("row", "col")
    )
    nys_block = lax.dynamic_slice_in_dim(nystrom, lax.axis_index("row") * block_rows, block_rows, 0)
    kern_batch = kernel(centres, batch_feats)
    partial_pred = lax.dot_general(
        kern_batch,
        weights,
        (((0,), (0,)), ((), ())),
        precision=lax.Precision.HIGHEST,
        preferred_element_type=jnp.float32,
    )
    prediction = lax.psum(partial_pred, ("row", "col"))
    residual = prediction - targets
    gradient = product(kernel(nys_block, batch_feats), residual)
    mode_terms = lax.dot_general(
        eigvecs,
        gradient,
        (((0,), (0,)), ((), ())),
        precision=lax.Precision.HIGHEST,
        preferred_element_type=jnp.float32,
    )
    coeff = mode_scale[:, None] * lax.psum(mode_terms, "row")
    correction = lax.psum(product(eigvecs, coeff), "col")
    direct = product(kern_batch, residual)
    folded = direct - product(
        kernel(centres, nystrom), lax.all_gather(correction, "row", axis=0, tiled=True)
    )
    step = learning_rate * folded
    return (residual, step)


def solution(mesh):
    in_specs = (
        P(("row", "col"), None),
        P(("row", "col"), None),
        P(),
        P(),
        P(),
        P("row", "col"),
        P("col"),
    )
    out_specs = (P(), P(("row", "col"), None))
    return jax.shard_map(local, mesh=mesh, in_specs=in_specs, out_specs=out_specs, check_vma=False)
```

profile of v0, /device:TPU:0, one launch (start us, length us, event | category | flops | bytes accessed | tf_op | source)
XLA Modules:
  0.0 467.1 jit_solution(167002956576013100)
XLA Ops:
  7.2 0.0 all-reduce.5.cloned.1.call-start
  7.2 0.7 compare_and_fusion.2
  8.0 1.4 copy.9
  9.4 1.0 gather_fusion
  10.4 0.9 select_select_fusion.1
  11.3 0.0 all-reduce.5.cloned.1.call-update
  11.4 0.0 all-reduce.9.cloned.1.call-start
  11.5 14.2 %gather_fusion.1 = f32[4096,64]{1,0:T(8,128)} fusion(f32[2048,64]{1,0:T(8,128)S(1)} %copy.9, s32[4096]{0:T(1024)S(1)} %fusion.30), kind=kCustom, calls=%fused_computation.1 | custom fusion | bytes 2113536 | tf_op jit(solution)/shard_map/jit(_take)/gather | solution.py:32
  25.7 6.0 %select_select_fusion = f32[4096,64]{1,0:T(8,128)} fusion(f32[4096,64]{1,0:T(8,128)} %gather_fusion.1, pred[4096]{0:T(1024)(128)(4,1)S(1)} %get-tuple-element.7, pred[4096]{0:T(1024)(128)(4,1)S(1)} %get-tuple-element.6), kind=kLoop, calls=%fused_computation.27 | loop fusion | flops 524288 | bytes 2105344 | tf_op jit(solution)/shard_map/jit(_where)/select_n | solution.py:33
  31.7 0.1 multiply_reduce_fusion.2
  31.8 111.6 %all-reduce.5.cloned.1.call-done = f32[512,64]{1,0:T(8,128)} async-done(((f32[512,64]{1,0:T(8,128)}), f32[512,64]{1,0:T(8,128)}) %all-reduce.5.cloned.1.call-update) | async-done | bytes 131088 | tf_op jit(solution)/shard_map/psum | solution.py:35
  143.3 1.1 multiply_reduce_fusion.3
  144.4 5.1 %fusion.13 = f32[2048,512]{0,1:T(8,128)S(1)} fusion(f32[512,64]{1,0:T(8,128)} %all-reduce.5.cloned.1.call-done, f32[2048,64]{0,1:T(8,128)S(1)} %copy-done.3, f32[512]{0:T(512)S(1)} %multiply_reduce_fusion.3, f32[2048]{0:T(1024)S(1)} %multiply_reduce_fusion.2), kind=kOutput, calls=%fused_computation.16 | convolution fusion | flops 810549248 | bytes 4859904 | tf_op jit(solution)/shard_map/dot_general | solution.py:12
  149.5 2.0 copy-done.1
  151.6 4.8 %fusion.36 = f32[512,64]{0,1:T(8,128)} fusion(f32[2048,512]{0,1:T(8,128)S(1)} %fusion.13, f32[2048,64]{0,1:T(8,128)S(1)} %copy-done.5), kind=kOutput, calls=%fused_computation.55 | convolution fusion | flops 805306368 | bytes 4849664 | tf_op jit(solution)/shard_map/dot_general | solution.py:40
  156.4 0.2 all-reduce.7.cloned.1.call-start
  156.7 134.4 %all-reduce.9.cloned.1.call-done = (f32[512,64]{0,1:T(8,128)}, f32[4096,64]{1,0:T(8,128)}) async-done(((f32[512,64]{0,1:T(8,128)}, f32[4096,64]{1,0:T(8,128)}), (f32[512,64]{0,1:T(8,128)}, f32[4096,64]{1,0:T(8,128)})) %all-reduce.9.cloned.1.call-update) | async-done | bytes 1179664 | tf_op jit(solution)/shard_map/psum | solution.py:47
  291.1 0.9 sub.30
  292.0 1.3 multiply_reduce_fusion.1
  293.3 2.8 fusion.26
  296.2 2.1 fusion.15
  298.3 1.0 convolution_bitcast_fusion.1
  299.3 10.7 %psum.38 = f32[128,64]{1,0:T(8,128)S(1)} all-reduce(f32[128,64]{1,0:T(8,128)S(1)} %convolution_bitcast_fusion.1), channel_id=1, replica_groups=mesh['row'=4,'col'=8] {'row'}, use_global_device_ids=true, to_apply=%region_7.8 | all-reduce | flops 8192 | bytes 65536 | tf_op jit(solution)/shard_map/psum | solution.py:57
  310.0 1.5 convolution_bitcast_fusion
  311.4 0.0 all-reduce.7.cloned.1.call-update
  311.5 0.3 all-gather.2.cloned.1.call-start
  311.8 0.6 multiply_reduce_fusion
  312.4 69.5 %all-reduce.7.cloned.1.call-done = f32[1024,64]{0,1:T(8,128)} async-done(((f32[1024,64]{0,1:T(8,128)}), f32[1024,64]{0,1:T(8,128)}) %all-reduce.7.cloned.1.call-update) | async-done | bytes 262160 | tf_op jit(solution)/shard_map/psum | solution.py:58
  381.9 0.0 all-gather.2.cloned.1.call-update
  381.9 30.2 %fusion.37 = f32[4096,2048]{0,1:T(8,128)} fusion(f32[4096,64]{1,0:T(8,128)S(1)} %copy-done.2, f32[2048,64]{0,1:T(8,128)S(1)} %copy-done.3), kind=kOutput, calls=%fused_computation.56 | convolution fusion | flops 6442450944 | bytes 35127296 | tf_op jit(solution)/shard_map/dot_general | solution.py:12
  412.1 42.7 %fusion.3 = f32[2048,64]{0,1:T(8,128)S(1)} fusion(f32[4096,64]{0,1:T(8,128)} %all-gather.2.cloned.1.call-done, f32[4096,2048]{0,1:T(8,128)} %fusion.37, f32[4096]{0:T(1024)S(1)} %multiply_reduce_fusion, f32[2048]{0:T(1024)S(1)} %multiply_reduce_fusion.2), kind=kOutput, calls=%fused_computation.6 | convolution fusion | flops 6484393984 | bytes 35151872 | tf_op jit(solution)/shard_map/dot_general | solution.py:21
  454.8 5.8 %fusion.14 = f32[2048,64]{0,1:T(8,128)} fusion(f32[2048,64]{0,1:T(8,128)S(1)} %fusion.3, f32[2048,512]{0,1:T(8,128)} %copy-done.1, f32[512,64]{0,1:T(8,128)S(1)} %sub.30), kind=kOutput, calls=%fused_computation.18 | convolution fusion | flops 805568512 | bytes 5373952 | tf_op jit(solution)/shard_map/dot_general | solution.py:21
  (24 shorter events, 0.1 us)
Async XLA Ops:
  7.2 291.1 %copy-start = (f32[1024,128]{1,0:T(8,128)S(1)}, f32[1024,128]{1,0:T(8,128)}, u32[]{:S(2)}) copy-start(f32[1024,128]{1,0:T(8,128)} %param.12) | copy-start | bytes 1572868
  7.2 136.2 %all-reduce.5.cloned.1.call-start = ((), (), s32[]{:S(2)}) async-start(), calls=%async_computation | async-start | bytes 524288 | tf_op jit(solution)/shard_map/psum | solution.py:35
  8.0 3.4 copy-start.8
  11.4 279.7 %all-reduce.9.cloned.1.call-start = ((), (), s32[]{:S(2)}) async-start(), calls=%async_computation.3 | async-start | bytes 4456448 | tf_op jit(solution)/shard_map/psum | solution.py:47
  25.7 6.0 %copy-start.3 = (f32[2048,64]{0,1:T(8,128)S(1)}, f32[2048,64]{0,1:T(8,128)}, u32[]{:S(2)}) copy-start(f32[2048,64]{0,1:T(8,128)} %param.7) | copy-start | bytes 1572868
  144.4 7.1 %copy-start.5 = (f32[2048,64]{0,1:T(8,128)S(1)}, f32[2048,64]{0,1:T(8,128)}, u32[]{:S(2)}) copy-start(f32[2048,64]{0,1:T(8,128)} %param.8) | copy-start | bytes 1572868
  149.5 2.0 copy-start.1
  156.4 134.7 %copy-start.7 = (f32[512,64]{0,1:T(8,128)S(1)}, f32[512,64]{0,1:T(8,128)}, u32[]{:S(2)}) copy-start(f32[512,64]{0,1:T(8,128)} %param.9) | copy-start | bytes 393220
  156.4 136.9 %copy-start.4 = (f32[512,64]{1,0:T(8,128)S(1)}, f32[512,64]{1,0:T(8,128)}, u32[]{:S(2)}) copy-start(f32[512,64]{1,0:T(8,128)} %all-reduce.5.cloned.1.call-done) | copy-start | bytes 393220
  156.4 225.5 %all-reduce.7.cloned.1.call-start = ((), (), s32[]{:S(2)}) async-start(), calls=%async_computation.1 | async-start | bytes 524288 | tf_op jit(solution)/shard_map/psum | solution.py:58
  292.0 162.8 %copy-start.6 = (f32[512,64]{0,1:T(8,128)}, f32[512,64]{0,1:T(8,128)S(1)}, u32[]{:S(2)}) copy-start(f32[512,64]{0,1:T(8,128)S(1)} %sub.30) | copy-start | bytes 393220
  296.2 13.8 %copy-start.9 = (f32[128]{0:T(128)S(1)}, f32[128]{0:T(128)}, u32[]{:S(2)}) copy-start(f32[128]{0:T(128)} %param.13) | copy-start | bytes 1540
  296.2 15.5 %copy-start.2 = (f32[4096,64]{1,0:T(8,128)S(1)}, f32[4096,64]{1,0:T(8,128)}, u32[]{:S(2)}) copy-start(f32[4096,64]{1,0:T(8,128)} %get-tuple-element.3) | copy-start | bytes 3145732
  311.5 100.6 %all-gather.2.cloned.1.call-start = ((), (), s32[]{:S(2)}) async-start(), calls=%async_computation.2 | async-start | bytes 1310720 | tf_op jit(solution)/shard_map/all_gather | solution.py:61
Sparse Core Ops, SparseCore 0:
  14.1 129.2 all-reduce.4
  156.6 134.4 all-reduce.8
  311.6 70.2 all-reduce.6
  383.3 15.8 all-gather.1
where the time goes:
time: 468 us; the launch traced here: 467 us
  waiting for transfers between devices  316 us (68%)
  matrix products  95.9 us (20%)
  local copies, waits for them, and re-layouts  18.7 us (4%)
  between operations  14 us (3%)
  other arithmetic  11.7 us (2%)
  blocking collectives  10.7 us (2%)
    psum x1, waiting for transfers between devices, local(): prediction = lax.psum(partial_pred, ('row', 'col'))  134 us
    psum x1, waiting for transfers between devices, local(): lax.psum((select_rows(batch_index), select_rows(nystrom_index)), ('row',...  112 us
    psum x1, waiting for transfers between devices, local(): correction = lax.psum(product(eigvecs, coeff), 'col')  69.5 us
    dot_general x4, matrix products, product(): jnp.dot(left, right, precision=lax.Precision.HIGHEST, preferred_element_t...  52 us
    dot_general x3, matrix products, kernel(): jnp.dot(left, right.T, precision=lax.Precision.HIGHEST, preferred_element...  38.1 us
    gather x2, local copies, waits for them, and re-layouts, select_rows(): fetched = jnp.take(centres, jnp.clip(local_rows, 0, rows_dev - 1), axis=0)  15.2 us
    psum x1, blocking collectives, local(): coeff = mode_scale[:, None] * lax.psum(mode_terms, 'row')  10.7 us
  transfers between devices with their start and end apart: 4, of which 3 were waited for; matrix products, arithmetic and copies ran while one was open for 11% of the time, Pallas kernels for 0%

commit v1 on v0

--- a/solution.py
+++ b/solution.py
@@ -4,6 +4,12 @@
 from jax.sharding import PartitionSpec as P
 
 learning_rate = 0.25
+
+
+def summed_here(block, axis):
+    pieces = lax.all_gather(block, axis, axis=0, tiled=False)
+    total = pieces.sum(axis=0)
+    return total
 
 
 def kernel(left, right):
@@ -44,7 +50,7 @@
         precision=lax.Precision.HIGHEST,
         preferred_element_type=jnp.float32,
     )
-    prediction = lax.psum(partial_pred, ("row", "col"))
+    prediction = summed_here(partial_pred, ("row", "col"))
     residual = prediction - targets
     gradient = product(kernel(nys_block, batch_feats), residual)
     mode_terms = lax.dot_general(

time: 468 us -> 425 us (0.908)
  waiting for transfers between devices: 316 us -> 265 us
  local copies, waits for them, and re-layouts: 18.7 us -> 24.1 us
    psum x1 -> x0, waiting for transfers between devices: 134 us -> none  [local(): prediction = lax.psum(partial_pred, ('row', 'col'))]
    all_gather x0 -> x1, waiting for transfers between devices: none -> 57.1 us  [summed_here(): pieces = lax.all_gather(block, axis, axis=0, tiled=False)]
    psum x1, waiting for transfers between devices: 112 us -> 139 us  [local(): lax.psum((select_rows(batch_index), select_rows(nystrom_index)), ('row',...]
    unnamed x21 -> x20, local copies, waits for them, and re-layouts: 3.47 us -> 8.94 us
  transfers between devices with their start and end apart: 4 -> 4, of which waited for: 3 -> 3; matrix products, arithmetic and copies ran while one was open for 11% -> 8% of each run, Pallas kernels for 0% -> 0%
where the time goes in v1:
time: 425 us; the launch traced here: 424 us
  waiting for transfers between devices  265 us (62%)
  matrix products  97.3 us (23%)
  local copies, waits for them, and re-layouts  24.1 us (6%)
  between operations  14 us (3%)
  blocking collectives  11.9 us (3%)
  other arithmetic  11.7 us (3%)
    psum x1, waiting for transfers between devices, local(): lax.psum((select_rows(batch_index), select_rows(nystrom_index)), ('row',...  139 us
    psum x1, waiting for transfers between devices, local(): correction = lax.psum(product(eigvecs, coeff), 'col')  69 us
    all_gather x1, waiting for transfers between devices, summed_here(): pieces = lax.all_gather(block, axis, axis=0, tiled=False)  57.1 us
    dot_general x4, matrix products, product(): jnp.dot(left, right, precision=lax.Precision.HIGHEST, preferred_element_t...  52 us
    dot_general x3, matrix products, kernel(): jnp.dot(left, right.T, precision=lax.Precision.HIGHEST, preferred_element...  38.3 us
    gather x2, local copies, waits for them, and re-layouts, select_rows(): fetched = jnp.take(centres, jnp.clip(local_rows, 0, rows_dev - 1), axis=0)  15.1 us
    psum x1, blocking collectives, local(): coeff = mode_scale[:, None] * lax.psum(mode_terms, 'row')  11.9 us
    unnamed x20, local copies, waits for them, and re-layouts  8.94 us
  transfers between devices with their start and end apart: 4, of which 3 were waited for; matrix products, arithmetic and copies ran while one was open for 8% of the time, Pallas kernels for 0%

profile of v1, /device:TPU:0, one launch (start us, length us, event | category | flops | bytes accessed | tf_op | source)
XLA Modules:
  0.0 424.2 jit_solution(8123085342271958507)
XLA Ops:
  7.2 0.8 compare_and_fusion.1
  8.0 0.7 fusion.30
  8.8 0.7 compare_and_fusion.2
  9.5 1.4 copy.9
  10.8 1.0 gather_fusion
  11.9 14.1 %gather_fusion.1 = f32[4096,64]{1,0:T(8,128)} fusion(f32[2048,64]{1,0:T(8,128)S(1)} %copy.9, s32[4096]{0:T(1024)S(1)} %fusion.30), kind=kCustom, calls=%fused_computation.1 | custom fusion | bytes 2113536 | tf_op jit(solution)/shard_map/jit(_take)/gather | solution.py:38
  26.0 0.9 select_select_fusion.1
  26.9 6.0 %select_select_fusion = f32[4096,64]{1,0:T(8,128)} fusion(f32[4096,64]{1,0:T(8,128)} %gather_fusion.1, pred[4096]{0:T(1024)(128)(4,1)S(1)} %get-tuple-element.7, pred[4096]{0:T(1024)(128)(4,1)S(1)} %get-tuple-element.6), kind=kLoop, calls=%fused_computation.28 | loop fusion | flops 524288 | bytes 2105344 | tf_op jit(solution)/shard_map/jit(_where)/select_n | solution.py:39
  32.9 0.1 multiply_reduce_fusion.2
  33.0 138.5 %all-reduce.6.cloned.1.call-done = (f32[512,64]{1,0:T(8,128)}, f32[4096,64]{1,0:T(8,128)}) async-done(((f32[512,64]{1,0:T(8,128)}, f32[4096,64]{1,0:T(8,128)}), (f32[512,64]{1,0:T(8,128)}, f32[4096,64]{1,0:T(8,128)})) %all-reduce.6.cloned.1.call-update) | async-done | bytes 1179664 | tf_op jit(solution)/shard_map/psum | solution.py:41
  171.5 1.1 multiply_reduce_fusion.3
  172.6 5.2 %fusion.13 = f32[2048,512]{0,1:T(8,128)S(1)} fusion(f32[512,64]{1,0:T(8,128)} %get-tuple-element.2, f32[2048,64]{0,1:T(8,128)S(1)} %copy-done.3, f32[512]{0:T(512)S(1)} %multiply_reduce_fusion.3, f32[2048]{0:T(1024)S(1)} %multiply_reduce_fusion.2), kind=kOutput, calls=%fused_computation.17 | convolution fusion | flops 810549248 | bytes 4859904 | tf_op jit(solution)/shard_map/dot_general | solution.py:18
  177.8 2.0 copy-done.1
  179.8 5.9 %fusion.36 = f32[512,64]{0,1:T(8,128)} fusion(f32[2048,512]{0,1:T(8,128)S(1)} %fusion.13, f32[2048,64]{0,1:T(8,128)} %param.8), kind=kOutput, calls=%fused_computation.56 | convolution fusion | flops 805306368 | bytes 4849664 | tf_op jit(solution)/shard_map/dot_general | solution.py:46
  185.8 0.2 all-reduce.4.cloned.1.call-start
  186.0 0.2 multiply_reduce_fusion.1
  186.2 3.1 fusion.26
  189.4 57.1 %all-gather.6.cloned.1.call-done = f32[16384,64]{0,1:T(8,128)} async-done(((f32[512,64]{0,1:T(8,128)}), f32[16384,64]{0,1:T(8,128)}) %all-gather.6.cloned.1.call-update) | async-done | bytes 4194320 | tf_op jit(solution)/shard_map/all_gather | solution.py:10
  246.5 4.6 %copy.11 = f32[8,8,32,512]{3,2,1,0:T(8,128)S(1)} copy(f32[8,8,32,512]{3,1,2,0:T(8,128)} %bitcast.40) | data formatting | bytes 8388608
  251.1 0.7 bitcast_reduce_fusion
  251.8 0.2 copy-done.7
  252.0 0.7 copy-done.4
  252.7 2.1 fusion.15
  254.8 1.0 convolution_bitcast_fusion.1
  255.8 11.9 %psum.30 = f32[128,64]{1,0:T(8,128)S(1)} all-reduce(f32[128,64]{1,0:T(8,128)S(1)} %convolution_bitcast_fusion.1), channel_id=1, replica_groups=mesh['row'=4,'col'=8] {'row'}, use_global_device_ids=true, to_apply=%region_7.8 | all-reduce | flops 8192 | bytes 65536 | tf_op jit(solution)/shard_map/psum | solution.py:63
  267.7 1.5 convolution_bitcast_fusion
  269.2 0.3 all-gather.4.cloned.1.call-start
  269.5 0.6 multiply_reduce_fusion
  270.1 69.0 %all-reduce.4.cloned.1.call-done = f32[1024,64]{0,1:T(8,128)} async-done(((f32[1024,64]{0,1:T(8,128)}), f32[1024,64]{0,1:T(8,128)}) %all-reduce.4.cloned.1.call-update) | async-done | bytes 262160 | tf_op jit(solution)/shard_map/psum | solution.py:64
  339.1 30.1 %fusion.37 = f32[4096,2048]{0,1:T(8,128)} fusion(f32[4096,64]{1,0:T(8,128)S(1)} %copy-done.2, f32[2048,64]{0,1:T(8,128)S(1)} %copy-done.3), kind=kOutput, calls=%fused_computation.57 | convolution fusion | flops 6442450944 | bytes 35127296 | tf_op jit(solution)/shard_map/dot_general | solution.py:18
  369.1 42.7 %fusion.3 = f32[2048,64]{0,1:T(8,128)S(1)} fusion(f32[4096,64]{0,1:T(8,128)} %all-gather.4.cloned.1.call-done, f32[4096,2048]{0,1:T(8,128)} %fusion.37, f32[4096]{0:T(1024)S(1)} %multiply_reduce_fusion, f32[2048]{0:T(1024)S(1)} %multiply_reduce_fusion.2), kind=kOutput, calls=%fused_computation.6 | convolution fusion | flops 6484393984 | bytes 35151872 | tf_op jit(solution)/shard_map/dot_general | solution.py:27
  411.9 5.8 %fusion.14 = f32[2048,64]{0,1:T(8,128)} fusion(f32[2048,64]{0,1:T(8,128)S(1)} %fusion.3, f32[2048,512]{0,1:T(8,128)} %copy-done.1, f32[512,64]{0,1:T(8,128)S(1)} %sub.30), kind=kOutput, calls=%fused_computation.19 | convolution fusion | flops 805568512 | bytes 5373952 | tf_op jit(solution)/shard_map/dot_general | solution.py:27
  (24 shorter events, 0.2 us)
Async XLA Ops:
  7.2 247.6 %copy-start = (f32[1024,128]{1,0:T(8,128)S(1)}, f32[1024,128]{1,0:T(8,128)}, u32[]{:S(2)}) copy-start(f32[1024,128]{1,0:T(8,128)} %param.12) | copy-start | bytes 1572868
  7.2 164.4 %all-reduce.6.cloned.1.call-start = ((), (), s32[]{:S(2)}) async-start(), calls=%async_computation.3 | async-start | bytes 4718592 | tf_op jit(solution)/shard_map/psum | solution.py:41
  26.0 6.9 %copy-start.3 = (f32[2048,64]{0,1:T(8,128)S(1)}, f32[2048,64]{0,1:T(8,128)}, u32[]{:S(2)}) copy-start(f32[2048,64]{0,1:T(8,128)} %param.7) | copy-start | bytes 1572868
  32.9 213.6 %all-gather.6.cloned.1.call-start = ((), (), s32[]{:S(2)}) async-start(), calls=%async_computation.2 | async-start | bytes 4325376 | tf_op jit(solution)/shard_map/all_gather | solution.py:10
  172.6 13.4 %copy-start.2 = (f32[4096,64]{1,0:T(8,128)S(1)}, f32[4096,64]{1,0:T(8,128)}, u32[]{:S(2)}) copy-start(f32[4096,64]{1,0:T(8,128)} %get-tuple-element.3) | copy-start | bytes 3145732
  177.8 2.0 copy-start.1
  179.8 6.4 %copy-start.5 = (f32[512,64]{1,0:T(8,128)S(1)}, f32[512,64]{1,0:T(8,128)}, u32[]{:S(2)}) copy-start(f32[512,64]{1,0:T(8,128)} %get-tuple-element.2) | copy-start | bytes 393220
  185.8 153.3 %all-reduce.4.cloned.1.call-start = ((), (), s32[]{:S(2)}) async-start(), calls=%async_computation | async-start | bytes 524288 | tf_op jit(solution)/shard_map/psum | solution.py:64
  251.1 0.9 copy-start.7
  251.1 1.7 copy-start.4
  251.1 16.6 %copy-start.8 = (f32[128]{0:T(128)S(1)}, f32[128]{0:T(128)}, u32[]{:S(2)}) copy-start(f32[128]{0:T(128)} %param.13) | copy-start | bytes 1540
  252.7 159.1 %copy-start.6 = (f32[512,64]{0,1:T(8,128)}, f32[512,64]{0,1:T(8,128)S(1)}, u32[]{:S(2)}) copy-start(f32[512,64]{0,1:T(8,128)S(1)} %sub.30) | copy-start | bytes 393220
  269.2 99.9 %all-gather.4.cloned.1.call-start = ((), (), s32[]{:S(2)}) async-start(), calls=%async_computation.1 | async-start | bytes 1310720 | tf_op jit(solution)/shard_map/all_gather | solution.py:67
Sparse Core Ops, SparseCore 0:
  33.0 138.4 all-reduce.5
  185.9 60.5 all-gather.5
  269.3 69.6 all-reduce.3
  340.5 15.8 all-gather.3
